TPU v7x, 512 devices: a whole 4x4x16 slice. The times are simulated.
512 devices in a mesh: tm: 16 (over z_hi, y), lat: 32 (over x, z_lo, core).
Axes of the slice: x: 4, y: 4, z: 16 (z_hi: 4, z_lo: 4; z = z_hi * 4 + z_lo), core: 2. Of those that a mesh axis runs over, the one named last changes fastest.
Arguments:
- cotangent: float32 [64, 512, 2048], P('tm', 'lat'), may hold values from -6 to 6
- iterates: float32 [3, 64, 512, 2048], P(None, 'tm', 'lat'), may hold values from -6 to 6
- range_field: float32 [512, 2048], P('lat', 'tm'), may hold values from 0.05 to 1
Outputs:
- noise_cotangent: float32 [64, 512, 2048], P('tm', 'lat')
- range_gradient: float32 [512, 2048], P('lat', 'tm')
All inputs are finite; a program needn't handle non-finite values.
Results may differ from a plain program's by a relative error of at most 0.0001.
Values sent between devices are 32-bit elements; how exact they have to be, the bound alone decides.
A program may use at most 64 MiB of HBM per device.

v0:
```python
import math
import jax
import jax.numpy as jnp
from jax import lax
from jax.sharding import PartitionSpec as P


def extended(cells, sides, width):
    for axis, dim in sides:
        count = lax.axis_size(axis)
        ends = count - 1
        head = lax.slice_in_dim(cells, 0, width, axis=dim)
        tail = lax.slice_in_dim(cells, cells.shape[dim] - width, cells.shape[dim], axis=dim)
        cells = jnp.concatenate(
            [
                lax.ppermute(tail, axis, [(i, (i + 1) % count) for i in range(ends)]),
                cells,
                lax.ppermute(head, axis, [((i + 1) % count, i) for i in range(ends)]),
            ],
            axis=dim,
        )
    return cells


def step_weights():
    centre_value = 6.525
    spread_value = 6.475
    root_order = (3, 0, 2, 1)
    return [
        1.0 / (centre_value + spread_value * math.cos(math.pi * (2 * section + 1) / 8.0))
        for section in root_order
    ]


def stencil(field, coefficient, previous, following, upper_row, lower_row):
    longitude = jnp.roll(field, 1, 2) + jnp.roll(field, -1, 2)
    return (
        (coefficient[None, :, :] + 6.0) * field
        - upper_row
        - lower_row
        - longitude
        - previous
        - following
    )


def body(cotangent, iterates, range_field):
    weights = step_weights()
    range_rows = lax.all_gather(range_field, "tm", axis=1, tiled=True)
    adjoint = cotangent
    noise_cot = weights[3] * cotangent
    gradient = jnp.zeros(range_field.shape, jnp.float32)
    for section in (3, 2, 1):
        own_cells = adjoint
        product_sum = -weights[section] * jnp.sum(own_cells * iterates[section - 1], axis=0)
        gradient = gradient + lax.psum_scatter(product_sum, "tm", scatter_dimension=1, tiled=True)
        timed = extended(adjoint, (("tm", 0),), 1)
        rowed = extended(adjoint, (("lat", 1),), 1)
        applied = stencil(adjoint, range_rows, timed[:-2], timed[2:], rowed[:, 2:], rowed[:, :-2])
        adjoint = adjoint - weights[section] * applied
        noise_cot = noise_cot + weights[section - 1] * adjoint
    return (noise_cot, gradient)


def solution(mesh):
    placed = (P("tm", "lat", None), P(None, "tm", "lat", None), P("lat", "tm"))
    return jax.shard_map(
        body,
        mesh=mesh,
        in_specs=placed,
        out_specs=(P("tm", "lat", None), P("lat", "tm")),
        check_vma=False,
    )
```

profile of v0, /device:TPU:4, one launch (start us, length us, event | category | flops | bytes accessed | tf_op | source)
XLA Modules:
  0.0 247.6 jit_solution(584649050877484398)
XLA Ops:
  7.2 0.0 reduce-scatter.2.cloned.1.call-start
  7.2 1.1 fusion.37
  8.4 5.9 %collective-permute-start = (f32[4,1,2048]{2,1,0:T(1,128)S(1)}, f32[4,1,2048]{2,1,0:T(1,128)S(1)}, u32[]{:S(2)}, u32[]{:S(2)}) collective-permute-start(f32[4,1,2048]{2,1,0:T(1,128)S(1)} %get-tuple-element.26), channel_id=1, source_target_pairs={{1,0},{2,1},{3,2},{4,3},{5,4},{6,5},{7,6},{8,7},{9,8},{10,9},{11,1... | collective-permute-start | bytes 98312 | tf_op jit(solution)/shard_map/ppermute | solution.py:18
  14.3 1.9 collective-permute-start.1
  16.2 1.0 fusion.38
  17.2 3.5 %collective-permute-start.2 = (f32[1,16,2048]{2,1,0:T(8,128)S(1)}, f32[1,16,2048]{2,1,0:T(8,128)S(1)}, u32[]{:S(2)}, u32[]{:S(2)}) collective-permute-start(f32[1,16,2048]{2,1,0:T(8,128)S(1)} %get-tuple-element.28), channel_id=1, source_target_pairs={{0,32},{32,64},{64,96},{96,128},{128,160},{160,192},{192,224},{224... | collective-permute-start | bytes 393224 | tf_op jit(solution)/shard_map/ppermute | solution.py:16
  20.7 1.3 collective-permute-start.3
  22.0 1.4 fusion.35
  23.4 58.1 %all_gather.3 = f32[16,2048]{1,0:T(8,128)S(1)} all-gather(f32[16,128]{1,0:T(8,128)S(1)} %copy-done.2), channel_id=1, replica_groups=mesh['tm'=16,'lat'=32] {'tm'}, dimensions={1}, use_global_device_ids=true | all-gather | bytes 139264 | tf_op jit(solution)/shard_map/all_gather | solution.py:49
  81.6 0.1 fusion.36
  81.7 0.3 fusion.18
  82.1 0.2 fusion.33
  82.3 2.0 collective-permute-start.4
  84.4 2.4 collective-permute-start.5
  86.8 1.3 collective-permute-start.6
  88.1 1.3 collective-permute-start.7
  89.4 0.1 fusion.32
  89.5 2.8 %collective-permute-done.5 = f32[4,1,2048]{2,1,0:T(1,128)S(1)} collective-permute-done((f32[4,1,2048]{2,1,0:T(1,128)S(1)}, f32[4,1,2048]{2,1,0:T(1,128)S(1)}, u32[]{:S(2)}, u32[]{:S(2)}) %collective-permute-start.5) | collective-permute-done | bytes 32800 | tf_op jit(solution)/shard_map/ppermute | solution.py:16
  92.3 3.1 %collective-permute-done.7 = f32[1,16,2048]{2,1,0:T(8,128)S(1)} collective-permute-done((f32[1,16,2048]{2,1,0:T(8,128)S(1)}, f32[1,16,2048]{2,1,0:T(8,128)S(1)}, u32[]{:S(2)}, u32[]{:S(2)}) %collective-permute-start.7) | collective-permute-done | bytes 131104 | tf_op jit(solution)/shard_map/ppermute | solution.py:18
  95.4 0.5 fusion.25
  96.0 0.2 fusion.27
  96.2 4.3 %collective-permute-start.8 = (f32[4,1,2048]{2,1,0:T(1,128)S(1)}, f32[4,1,2048]{2,1,0:T(1,128)S(1)}, u32[]{:S(2)}, u32[]{:S(2)}) collective-permute-start(f32[4,1,2048]{2,1,0:T(1,128)S(1)} %get-tuple-element.10), channel_id=1, source_target_pairs={{1,0},{2,1},{3,2},{4,3},{5,4},{6,5},{7,6},{8,7},{9,8},{10,9},{11,1... | collective-permute-start | bytes 98312 | tf_op jit(solution)/shard_map/ppermute | solution.py:18
  100.5 1.9 collective-permute-start.9
  102.4 4.9 %collective-permute-start.10 = (f32[1,16,2048]{2,1,0:T(8,128)S(1)}, f32[1,16,2048]{2,1,0:T(8,128)S(1)}, u32[]{:S(2)}, u32[]{:S(2)}) collective-permute-start(f32[1,16,2048]{2,1,0:T(8,128)S(1)} %get-tuple-element.12), channel_id=1, source_target_pairs={{0,32},{32,64},{64,96},{96,128},{128,160},{160,192},{192,224},{224... | collective-permute-start | bytes 393224 | tf_op jit(solution)/shard_map/ppermute | solution.py:16
  107.3 1.3 collective-permute-start.11
  108.6 0.7 add_add_fusion
  109.3 0.1 fusion.28
  109.4 0.0 reduce-scatter.2.cloned.1.call-update
  109.4 4.2 %collective-permute-done.9 = f32[4,1,2048]{2,1,0:T(1,128)S(1)} collective-permute-done((f32[4,1,2048]{2,1,0:T(1,128)S(1)}, f32[4,1,2048]{2,1,0:T(1,128)S(1)}, u32[]{:S(2)}, u32[]{:S(2)}) %collective-permute-start.9) | collective-permute-done | bytes 32800 | tf_op jit(solution)/shard_map/ppermute | solution.py:16
  113.6 6.9 %collective-permute-done.11 = f32[1,16,2048]{2,1,0:T(8,128)S(1)} collective-permute-done((f32[1,16,2048]{2,1,0:T(8,128)S(1)}, f32[1,16,2048]{2,1,0:T(8,128)S(1)}, u32[]{:S(2)}, u32[]{:S(2)}) %collective-permute-start.11) | collective-permute-done | bytes 131104 | tf_op jit(solution)/shard_map/ppermute | solution.py:18
  120.5 1.2 fusion.4
  121.7 119.0 %reduce-scatter.2.cloned.1.call-done = f32[16,128]{1,0:T(8,128)} async-done(((f32[16,2048]{1,0:T(8,128)}), f32[16,128]{1,0:T(8,128)}) %reduce-scatter.2.cloned.1.call-update) | async-done | bytes 8208 | tf_op jit(solution)/shard_map/reduce_scatter | solution.py:56
  (19 shorter events, 0.2 us)
Async XLA Ops:
  7.2 74.4 %copy-start = (f32[4,16,2048]{2,1,0:T(8,128)S(1)}, f32[4,16,2048]{2,1,0:T(8,128)}, u32[]{:S(2)}) copy-start(f32[4,16,2048]{2,1,0:T(8,128)} %param.3) | copy-start | bytes 1572868
  7.2 16.3 %copy-start.2 = (f32[16,128]{1,0:T(8,128)S(1)}, f32[16,128]{1,0:T(8,128)}, u32[]{:S(2)}) copy-start(f32[16,128]{1,0:T(8,128)} %param.5) | copy-start | bytes 24580
  7.2 233.5 %reduce-scatter.2.cloned.1.call-start = ((), (), s32[]{:S(2)}) async-start(), calls=%async_computation.1 | async-start | bytes 139264 | tf_op jit(solution)/shard_map/reduce_scatter | solution.py:56
  8.4 73.3 %collective-permute-start = (f32[4,1,2048]{2,1,0:T(1,128)S(1)}, f32[4,1,2048]{2,1,0:T(1,128)S(1)}, u32[]{:S(2)}, u32[]{:S(2)}) collective-permute-start(f32[4,1,2048]{2,1,0:T(1,128)S(1)} %get-tuple-element.26), channel_id=1, source_target_pairs={{1,0},{2,1},{3,2},{4,3},{5,4},{6,5},{7,6},{8,7},{9,8},{10,9},{11,1... | collective-permute-start | bytes 98312 | tf_op jit(solution)/shard_map/ppermute | solution.py:18
  14.3 67.3 %collective-permute-start.1 = (f32[4,1,2048]{2,1,0:T(1,128)S(1)}, f32[4,1,2048]{2,1,0:T(1,128)S(1)}, u32[]{:S(2)}, u32[]{:S(2)}) collective-permute-start(f32[4,1,2048]{2,1,0:T(1,128)S(1)} %get-tuple-element.27), channel_id=1, source_target_pairs={{0,1},{1,2},{2,3},{3,4},{4,5},{5,6},{6,7},{7,8},{8,9},{9,10},{10,1... | collective-permute-start | bytes 98312 | tf_op jit(solution)/shard_map/ppermute | solution.py:16
  17.2 64.4 %collective-permute-start.2 = (f32[1,16,2048]{2,1,0:T(8,128)S(1)}, f32[1,16,2048]{2,1,0:T(8,128)S(1)}, u32[]{:S(2)}, u32[]{:S(2)}) collective-permute-start(f32[1,16,2048]{2,1,0:T(8,128)S(1)} %get-tuple-element.28), channel_id=1, source_target_pairs={{0,32},{32,64},{64,96},{96,128},{128,160},{160,192},{192,224},{224... | collective-permute-start | bytes 393224 | tf_op jit(solution)/shard_map/ppermute | solution.py:16
  20.7 60.9 %collective-permute-start.3 = (f32[1,16,2048]{2,1,0:T(8,128)S(1)}, f32[1,16,2048]{2,1,0:T(8,128)S(1)}, u32[]{:S(2)}, u32[]{:S(2)}) collective-permute-start(f32[1,16,2048]{2,1,0:T(8,128)S(1)} %get-tuple-element.29), channel_id=1, source_target_pairs={{32,0},{64,32},{96,64},{128,96},{160,128},{192,160},{224,192},{256... | collective-permute-start | bytes 393224 | tf_op jit(solution)/shard_map/ppermute | solution.py:18
  82.0 13.4 %copy-start.1 = (f32[3,4,16,2048]{3,2,1,0:T(8,128)S(1)}, f32[3,4,16,2048]{3,2,1,0:T(8,128)}, u32[]{:S(2)}) copy-start(f32[3,4,16,2048]{3,2,1,0:T(8,128)} %param.4) | copy-start | bytes 4718596
  82.3 7.2 %collective-permute-start.4 = (f32[4,1,2048]{2,1,0:T(1,128)S(1)}, f32[4,1,2048]{2,1,0:T(1,128)S(1)}, u32[]{:S(2)}, u32[]{:S(2)}) collective-permute-start(f32[4,1,2048]{2,1,0:T(1,128)S(1)} %get-tuple-element.14), channel_id=1, source_target_pairs={{1,0},{2,1},{3,2},{4,3},{5,4},{6,5},{7,6},{8,7},{9,8},{10,9},{11,1... | collective-permute-start | bytes 98312 | tf_op jit(solution)/shard_map/ppermute | solution.py:18
  84.4 7.9 %collective-permute-start.5 = (f32[4,1,2048]{2,1,0:T(1,128)S(1)}, f32[4,1,2048]{2,1,0:T(1,128)S(1)}, u32[]{:S(2)}, u32[]{:S(2)}) collective-permute-start(f32[4,1,2048]{2,1,0:T(1,128)S(1)} %get-tuple-element.15), channel_id=1, source_target_pairs={{0,1},{1,2},{2,3},{3,4},{4,5},{5,6},{6,7},{7,8},{8,9},{9,10},{10,1... | collective-permute-start | bytes 98312 | tf_op jit(solution)/shard_map/ppermute | solution.py:16
  86.8 5.5 %collective-permute-start.6 = (f32[1,16,2048]{2,1,0:T(8,128)S(1)}, f32[1,16,2048]{2,1,0:T(8,128)S(1)}, u32[]{:S(2)}, u32[]{:S(2)}) collective-permute-start(f32[1,16,2048]{2,1,0:T(8,128)S(1)} %get-tuple-element.20), channel_id=1, source_target_pairs={{0,32},{32,64},{64,96},{96,128},{128,160},{160,192},{192,224},{224... | collective-permute-start | bytes 393224 | tf_op jit(solution)/shard_map/ppermute | solution.py:16
  88.1 7.3 %collective-permute-start.7 = (f32[1,16,2048]{2,1,0:T(8,128)S(1)}, f32[1,16,2048]{2,1,0:T(8,128)S(1)}, u32[]{:S(2)}, u32[]{:S(2)}) collective-permute-start(f32[1,16,2048]{2,1,0:T(8,128)S(1)} %get-tuple-element.21), channel_id=1, source_target_pairs={{32,0},{64,32},{96,64},{128,96},{160,128},{192,160},{224,192},{256... | collective-permute-start | bytes 393224 | tf_op jit(solution)/shard_map/ppermute | solution.py:18
  96.2 13.2 %collective-permute-start.8 = (f32[4,1,2048]{2,1,0:T(1,128)S(1)}, f32[4,1,2048]{2,1,0:T(1,128)S(1)}, u32[]{:S(2)}, u32[]{:S(2)}) collective-permute-start(f32[4,1,2048]{2,1,0:T(1,128)S(1)} %get-tuple-element.10), channel_id=1, source_target_pairs={{1,0},{2,1},{3,2},{4,3},{5,4},{6,5},{7,6},{8,7},{9,8},{10,9},{11,1... | collective-permute-start | bytes 98312 | tf_op jit(solution)/shard_map/ppermute | solution.py:18
  100.5 13.1 %collective-permute-start.9 = (f32[4,1,2048]{2,1,0:T(1,128)S(1)}, f32[4,1,2048]{2,1,0:T(1,128)S(1)}, u32[]{:S(2)}, u32[]{:S(2)}) collective-permute-start(f32[4,1,2048]{2,1,0:T(1,128)S(1)} %get-tuple-element.11), channel_id=1, source_target_pairs={{0,1},{1,2},{2,3},{3,4},{4,5},{5,6},{6,7},{7,8},{8,9},{9,10},{10,1... | collective-permute-start | bytes 98312 | tf_op jit(solution)/shard_map/ppermute | solution.py:16
  102.4 11.2 %collective-permute-start.10 = (f32[1,16,2048]{2,1,0:T(8,128)S(1)}, f32[1,16,2048]{2,1,0:T(8,128)S(1)}, u32[]{:S(2)}, u32[]{:S(2)}) collective-permute-start(f32[1,16,2048]{2,1,0:T(8,128)S(1)} %get-tuple-element.12), channel_id=1, source_target_pairs={{0,32},{32,64},{64,96},{96,128},{128,160},{160,192},{192,224},{224... | collective-permute-start | bytes 393224 | tf_op jit(solution)/shard_map/ppermute | solution.py:16
  107.3 13.1 %collective-permute-start.11 = (f32[1,16,2048]{2,1,0:T(8,128)S(1)}, f32[1,16,2048]{2,1,0:T(8,128)S(1)}, u32[]{:S(2)}, u32[]{:S(2)}) collective-permute-start(f32[1,16,2048]{2,1,0:T(8,128)S(1)} %get-tuple-element.13), channel_id=1, source_target_pairs={{32,0},{64,32},{96,64},{128,96},{160,128},{192,160},{224,192},{256... | collective-permute-start | bytes 393224 | tf_op jit(solution)/shard_map/ppermute | solution.py:18
Sparse Core Ops, SparseCore 0:
  109.6 131.1 reduce-scatter.1
where the time goes:
time: 248 us
  waiting for transfers between devices  136 us (55%)
  blocking collectives  58.1 us (23%)
  starting transfers between devices  32.1 us (13%)
  between operations  14.2 us (6%)
  local copies, waits for them, and re-layouts  4.31 us (2%)
  other arithmetic  2.77 us (1%)
    reduce_scatter x1, waiting for transfers between devices, body(): lax.psum_scatter(product_sum, 'tm', scatter_dimension=1, tiled=True)  119 us
    all_gather x1, blocking collectives, body(): range_rows = lax.all_gather(range_field, 'tm', axis=1, tiled=True)  58.1 us
    ppermute x6, starting transfers between devices, extended(): lax.ppermute(head, axis, [((i + 1) % count, i) for i in range(ends)])  16.1 us
    ppermute x6, starting transfers between devices, extended(): lax.ppermute(tail, axis, [(i, (i + 1) % count) for i in range(ends)])  16 us
    ppermute x6, waiting for transfers between devices, extended(): lax.ppermute(head, axis, [((i + 1) % count, i) for i in range(ends)])  9.98 us
    ppermute x6, waiting for transfers between devices, extended(): lax.ppermute(tail, axis, [(i, (i + 1) % count) for i in range(ends)])  7.01 us
  transfers between devices with their start and end apart: 13, of which 5 were waited for; matrix products, arithmetic and copies ran while one was open for 2% of the time, Pallas kernels for 0%

commit v1 on v0

--- a/solution.py
+++ b/solution.py
@@ -46,7 +46,10 @@
 
 def body(cotangent, iterates, range_field):
     weights = step_weights()
-    range_rows = lax.all_gather(range_field, "tm", axis=1, tiled=True)
+    devices = lax.axis_size("tm")
+    blocks = jnp.stack([range_field for _ in range(devices)])
+    blocks = lax.all_to_all(blocks, "tm", split_axis=0, concat_axis=0)
+    range_rows = jnp.concatenate(blocks, axis=1)
     adjoint = cotangent
     noise_cot = weights[3] * cotangent
     gradient = jnp.zeros(range_field.shape, jnp.float32)

time: 248 us -> 219 us (0.88)
  the two profiles are of different devices: /device:TPU:4 before, /device:TPU:2 now
where the time goes in v1:
time: 219 us
  waiting for transfers between devices  137 us (63%)
  starting transfers between devices  59.6 us (27%)
  between operations  14.2 us (6%)
  local copies, waits for them, and re-layouts  5.25 us (2%)
  other arithmetic  2.75 us (1%)
    reduce_scatter x1, waiting for transfers between devices, body(): lax.psum_scatter(product_sum, 'tm', scatter_dimension=1, tiled=True)  116 us
    ppermute x6, starting transfers between devices, extended(): lax.ppermute(tail, axis, [(i, (i + 1) % count) for i in range(ends)])  27.3 us
    ppermute x6, starting transfers between devices, extended(): lax.ppermute(head, axis, [((i + 1) % count, i) for i in range(ends)])  17.1 us
    all_to_all x1, starting transfers between devices, body(): blocks = lax.all_to_all(blocks, 'tm', split_axis=0, concat_axis=0)  15.1 us
    all_to_all x1, waiting for transfers between devices, body(): blocks = lax.all_to_all(blocks, 'tm', split_axis=0, concat_axis=0)  9.93 us
    ppermute x6, waiting for transfers between devices, extended(): lax.ppermute(head, axis, [((i + 1) % count, i) for i in range(ends)])  6.87 us
  transfers between devices with their start and end apart: 14, of which 6 were waited for; matrix products, arithmetic and copies ran while one was open for 3% of the time, Pallas kernels for 0%

profile of v1, /device:TPU:2, one launch (start us, length us, event | category | flops | bytes accessed | tf_op | source)
XLA Modules:
  0.0 218.6 jit_solution(6123142182191183341)
XLA Ops:
  7.2 1.1 fusion.37
  8.3 5.9 %collective-permute-start = (f32[4,1,2048]{2,1,0:T(1,128)S(1)}, f32[4,1,2048]{2,1,0:T(1,128)S(1)}, u32[]{:S(2)}, u32[]{:S(2)}) collective-permute-start(f32[4,1,2048]{2,1,0:T(1,128)S(1)} %get-tuple-element.26), channel_id=1, source_target_pairs={{1,0},{2,1},{3,2},{4,3},{5,4},{6,5},{7,6},{8,7},{9,8},{10,9},{11,1... | collective-permute-start | bytes 98312 | tf_op jit(solution)/shard_map/ppermute | solution.py:18
  14.3 1.9 collective-permute-start.1
  16.2 1.4 stack.2
  17.6 15.1 %all-to-all-start = ((f32[16,16,128]{2,1,0:T(8,128)}), f32[16,16,128]{2,1,0:T(8,128)S(1)}, u32[]{:S(2)}, u32[]{:S(2)}) async-start(f32[16,16,128]{2,1,0:T(8,128)} %stack.2), calls=%async_computation | async-start | bytes 262144 | tf_op jit(solution)/shard_map/all_to_all | solution.py:51
  32.7 1.0 fusion.38
  33.7 3.8 %collective-permute-start.2 = (f32[1,16,2048]{2,1,0:T(8,128)S(1)}, f32[1,16,2048]{2,1,0:T(8,128)S(1)}, u32[]{:S(2)}, u32[]{:S(2)}) collective-permute-start(f32[1,16,2048]{2,1,0:T(8,128)S(1)} %get-tuple-element.28), channel_id=1, source_target_pairs={{0,32},{32,64},{64,96},{96,128},{128,160},{160,192},{192,224},{224... | collective-permute-start | bytes 393224 | tf_op jit(solution)/shard_map/ppermute | solution.py:16
  37.6 1.3 collective-permute-start.3
  38.9 0.9 fusion.36
  39.7 0.2 fusion.35
  39.9 9.9 %all-to-all-done = f32[16,16,128]{2,1,0:T(8,128)S(1)} async-done(((f32[16,16,128]{2,1,0:T(8,128)}), f32[16,16,128]{2,1,0:T(8,128)S(1)}, u32[]{:S(2)}, u32[]{:S(2)}) %all-to-all-start) | async-done | bytes 131104 | tf_op jit(solution)/shard_map/all_to_all | solution.py:51
  49.9 0.3 fusion.18
  50.3 0.2 fusion.33
  50.5 3.1 %collective-permute-start.4 = (f32[4,1,2048]{2,1,0:T(1,128)S(1)}, f32[4,1,2048]{2,1,0:T(1,128)S(1)}, u32[]{:S(2)}, u32[]{:S(2)}) collective-permute-start(f32[4,1,2048]{2,1,0:T(1,128)S(1)} %get-tuple-element.14), channel_id=1, source_target_pairs={{1,0},{2,1},{3,2},{4,3},{5,4},{6,5},{7,6},{8,7},{9,8},{10,9},{11,1... | collective-permute-start | bytes 98312 | tf_op jit(solution)/shard_map/ppermute | solution.py:18
  53.6 1.9 collective-permute-start.5
  55.6 2.3 %collective-permute-start.6 = (f32[1,16,2048]{2,1,0:T(8,128)S(1)}, f32[1,16,2048]{2,1,0:T(8,128)S(1)}, u32[]{:S(2)}, u32[]{:S(2)}) collective-permute-start(f32[1,16,2048]{2,1,0:T(8,128)S(1)} %get-tuple-element.20), channel_id=1, source_target_pairs={{0,32},{32,64},{64,96},{96,128},{128,160},{160,192},{192,224},{224... | collective-permute-start | bytes 393224 | tf_op jit(solution)/shard_map/ppermute | solution.py:16
  57.8 1.3 collective-permute-start.7
  59.1 0.1 fusion.32
  59.2 3.8 %collective-permute-done.5 = f32[4,1,2048]{2,1,0:T(1,128)S(1)} collective-permute-done((f32[4,1,2048]{2,1,0:T(1,128)S(1)}, f32[4,1,2048]{2,1,0:T(1,128)S(1)}, u32[]{:S(2)}, u32[]{:S(2)}) %collective-permute-start.5) | collective-permute-done | bytes 32800 | tf_op jit(solution)/shard_map/ppermute | solution.py:16
  63.0 2.7 %collective-permute-done.7 = f32[1,16,2048]{2,1,0:T(8,128)S(1)} collective-permute-done((f32[1,16,2048]{2,1,0:T(8,128)S(1)}, f32[1,16,2048]{2,1,0:T(8,128)S(1)}, u32[]{:S(2)}, u32[]{:S(2)}) %collective-permute-start.7) | collective-permute-done | bytes 131104 | tf_op jit(solution)/shard_map/ppermute | solution.py:18
  65.7 0.5 fusion.25
  66.2 0.2 fusion.27
  66.4 4.2 %collective-permute-start.8 = (f32[4,1,2048]{2,1,0:T(1,128)S(1)}, f32[4,1,2048]{2,1,0:T(1,128)S(1)}, u32[]{:S(2)}, u32[]{:S(2)}) collective-permute-start(f32[4,1,2048]{2,1,0:T(1,128)S(1)} %get-tuple-element.10), channel_id=1, source_target_pairs={{1,0},{2,1},{3,2},{4,3},{5,4},{6,5},{7,6},{8,7},{9,8},{10,9},{11,1... | collective-permute-start | bytes 98312 | tf_op jit(solution)/shard_map/ppermute | solution.py:18
  70.6 1.9 collective-permute-start.9
  72.6 15.5 %collective-permute-start.10 = (f32[1,16,2048]{2,1,0:T(8,128)S(1)}, f32[1,16,2048]{2,1,0:T(8,128)S(1)}, u32[]{:S(2)}, u32[]{:S(2)}) collective-permute-start(f32[1,16,2048]{2,1,0:T(8,128)S(1)} %get-tuple-element.12), channel_id=1, source_target_pairs={{0,32},{32,64},{64,96},{96,128},{128,160},{160,192},{192,224},{224... | collective-permute-start | bytes 393224 | tf_op jit(solution)/shard_map/ppermute | solution.py:16
  88.1 1.3 collective-permute-start.11
  89.4 0.7 add_add_fusion
  90.0 0.1 fusion.28
  90.2 0.6 collective-permute-done.10
  90.7 4.2 %collective-permute-done.11 = f32[1,16,2048]{2,1,0:T(8,128)S(1)} collective-permute-done((f32[1,16,2048]{2,1,0:T(8,128)S(1)}, f32[1,16,2048]{2,1,0:T(8,128)S(1)}, u32[]{:S(2)}, u32[]{:S(2)}) %collective-permute-start.11) | collective-permute-done | bytes 131104 | tf_op jit(solution)/shard_map/ppermute | solution.py:18
  94.9 1.2 fusion.4
  96.2 115.6 %reduce-scatter.2.cloned.1.call-done = f32[16,128]{1,0:T(8,128)} async-done(((f32[16,2048]{1,0:T(8,128)}), f32[16,128]{1,0:T(8,128)}) %reduce-scatter.2.cloned.1.call-update) | async-done | bytes 8208 | tf_op jit(solution)/shard_map/reduce_scatter | solution.py:59
  (19 shorter events, 0.2 us)
Async XLA Ops:
  7.2 32.6 %copy-start = (f32[4,16,2048]{2,1,0:T(8,128)S(1)}, f32[4,16,2048]{2,1,0:T(8,128)}, u32[]{:S(2)}) copy-start(f32[4,16,2048]{2,1,0:T(8,128)} %param.3) | copy-start | bytes 1572868
  8.3 41.6 %collective-permute-start = (f32[4,1,2048]{2,1,0:T(1,128)S(1)}, f32[4,1,2048]{2,1,0:T(1,128)S(1)}, u32[]{:S(2)}, u32[]{:S(2)}) collective-permute-start(f32[4,1,2048]{2,1,0:T(1,128)S(1)} %get-tuple-element.26), channel_id=1, source_target_pairs={{1,0},{2,1},{3,2},{4,3},{5,4},{6,5},{7,6},{8,7},{9,8},{10,9},{11,1... | collective-permute-start | bytes 98312 | tf_op jit(solution)/shard_map/ppermute | solution.py:18
  14.3 35.6 %collective-permute-start.1 = (f32[4,1,2048]{2,1,0:T(1,128)S(1)}, f32[4,1,2048]{2,1,0:T(1,128)S(1)}, u32[]{:S(2)}, u32[]{:S(2)}) collective-permute-start(f32[4,1,2048]{2,1,0:T(1,128)S(1)} %get-tuple-element.27), channel_id=1, source_target_pairs={{0,1},{1,2},{2,3},{3,4},{4,5},{5,6},{6,7},{7,8},{8,9},{9,10},{10,1... | collective-permute-start | bytes 98312 | tf_op jit(solution)/shard_map/ppermute | solution.py:16
  17.6 32.3 %all-to-all-start = ((f32[16,16,128]{2,1,0:T(8,128)}), f32[16,16,128]{2,1,0:T(8,128)S(1)}, u32[]{:S(2)}, u32[]{:S(2)}) async-start(f32[16,16,128]{2,1,0:T(8,128)} %stack.2), calls=%async_computation | async-start | bytes 262144 | tf_op jit(solution)/shard_map/all_to_all | solution.py:51
  32.7 179.0 %reduce-scatter.2.cloned.1.call-start = ((), (), s32[]{:S(2)}) async-start(), calls=%async_computation.2 | async-start | bytes 139264 | tf_op jit(solution)/shard_map/reduce_scatter | solution.py:59
  33.7 16.2 %collective-permute-start.2 = (f32[1,16,2048]{2,1,0:T(8,128)S(1)}, f32[1,16,2048]{2,1,0:T(8,128)S(1)}, u32[]{:S(2)}, u32[]{:S(2)}) collective-permute-start(f32[1,16,2048]{2,1,0:T(8,128)S(1)} %get-tuple-element.28), channel_id=1, source_target_pairs={{0,32},{32,64},{64,96},{96,128},{128,160},{160,192},{192,224},{224... | collective-permute-start | bytes 393224 | tf_op jit(solution)/shard_map/ppermute | solution.py:16
  37.6 12.3 %collective-permute-start.3 = (f32[1,16,2048]{2,1,0:T(8,128)S(1)}, f32[1,16,2048]{2,1,0:T(8,128)S(1)}, u32[]{:S(2)}, u32[]{:S(2)}) collective-permute-start(f32[1,16,2048]{2,1,0:T(8,128)S(1)} %get-tuple-element.29), channel_id=1, source_target_pairs={{32,0},{64,32},{96,64},{128,96},{160,128},{192,160},{224,192},{256... | collective-permute-start | bytes 393224 | tf_op jit(solution)/shard_map/ppermute | solution.py:18
  50.2 15.4 %copy-start.1 = (f32[3,4,16,2048]{3,2,1,0:T(8,128)S(1)}, f32[3,4,16,2048]{3,2,1,0:T(8,128)}, u32[]{:S(2)}) copy-start(f32[3,4,16,2048]{3,2,1,0:T(8,128)} %param.4) | copy-start | bytes 4718596
  50.5 8.7 %collective-permute-start.4 = (f32[4,1,2048]{2,1,0:T(1,128)S(1)}, f32[4,1,2048]{2,1,0:T(1,128)S(1)}, u32[]{:S(2)}, u32[]{:S(2)}) collective-permute-start(f32[4,1,2048]{2,1,0:T(1,128)S(1)} %get-tuple-element.14), channel_id=1, source_target_pairs={{1,0},{2,1},{3,2},{4,3},{5,4},{6,5},{7,6},{8,7},{9,8},{10,9},{11,1... | collective-permute-start | bytes 98312 | tf_op jit(solution)/shard_map/ppermute | solution.py:18
  53.6 9.3 %collective-permute-start.5 = (f32[4,1,2048]{2,1,0:T(1,128)S(1)}, f32[4,1,2048]{2,1,0:T(1,128)S(1)}, u32[]{:S(2)}, u32[]{:S(2)}) collective-permute-start(f32[4,1,2048]{2,1,0:T(1,128)S(1)} %get-tuple-element.15), channel_id=1, source_target_pairs={{0,1},{1,2},{2,3},{3,4},{4,5},{5,6},{6,7},{7,8},{8,9},{9,10},{10,1... | collective-permute-start | bytes 98312 | tf_op jit(solution)/shard_map/ppermute | solution.py:16
  55.6 7.4 %collective-permute-start.6 = (f32[1,16,2048]{2,1,0:T(8,128)S(1)}, f32[1,16,2048]{2,1,0:T(8,128)S(1)}, u32[]{:S(2)}, u32[]{:S(2)}) collective-permute-start(f32[1,16,2048]{2,1,0:T(8,128)S(1)} %get-tuple-element.20), channel_id=1, source_target_pairs={{0,32},{32,64},{64,96},{96,128},{128,160},{160,192},{192,224},{224... | collective-permute-start | bytes 393224 | tf_op jit(solution)/shard_map/ppermute | solution.py:16
  57.8 7.8 %collective-permute-start.7 = (f32[1,16,2048]{2,1,0:T(8,128)S(1)}, f32[1,16,2048]{2,1,0:T(8,128)S(1)}, u32[]{:S(2)}, u32[]{:S(2)}) collective-permute-start(f32[1,16,2048]{2,1,0:T(8,128)S(1)} %get-tuple-element.21), channel_id=1, source_target_pairs={{32,0},{64,32},{96,64},{128,96},{160,128},{192,160},{224,192},{256... | collective-permute-start | bytes 393224 | tf_op jit(solution)/shard_map/ppermute | solution.py:18
  66.4 23.7 %collective-permute-start.8 = (f32[4,1,2048]{2,1,0:T(1,128)S(1)}, f32[4,1,2048]{2,1,0:T(1,128)S(1)}, u32[]{:S(2)}, u32[]{:S(2)}) collective-permute-start(f32[4,1,2048]{2,1,0:T(1,128)S(1)} %get-tuple-element.10), channel_id=1, source_target_pairs={{1,0},{2,1},{3,2},{4,3},{5,4},{6,5},{7,6},{8,7},{9,8},{10,9},{11,1... | collective-permute-start | bytes 98312 | tf_op jit(solution)/shard_map/ppermute | solution.py:18
  70.6 19.5 %collective-permute-start.9 = (f32[4,1,2048]{2,1,0:T(1,128)S(1)}, f32[4,1,2048]{2,1,0:T(1,128)S(1)}, u32[]{:S(2)}, u32[]{:S(2)}) collective-permute-start(f32[4,1,2048]{2,1,0:T(1,128)S(1)} %get-tuple-element.11), channel_id=1, source_target_pairs={{0,1},{1,2},{2,3},{3,4},{4,5},{5,6},{6,7},{7,8},{8,9},{9,10},{10,1... | collective-permute-start | bytes 98312 | tf_op jit(solution)/shard_map/ppermute | solution.py:16
  72.6 18.2 %collective-permute-start.10 = (f32[1,16,2048]{2,1,0:T(8,128)S(1)}, f32[1,16,2048]{2,1,0:T(8,128)S(1)}, u32[]{:S(2)}, u32[]{:S(2)}) collective-permute-start(f32[1,16,2048]{2,1,0:T(8,128)S(1)} %get-tuple-element.12), channel_id=1, source_target_pairs={{0,32},{32,64},{64,96},{96,128},{128,160},{160,192},{192,224},{224... | collective-permute-start | bytes 393224 | tf_op jit(solution)/shard_map/ppermute | solution.py:16
  88.1 6.9 %collective-permute-start.11 = (f32[1,16,2048]{2,1,0:T(8,128)S(1)}, f32[1,16,2048]{2,1,0:T(8,128)S(1)}, u32[]{:S(2)}, u32[]{:S(2)}) collective-permute-start(f32[1,16,2048]{2,1,0:T(8,128)S(1)} %get-tuple-element.13), channel_id=1, source_target_pairs={{32,0},{64,32},{96,64},{128,96},{160,128},{192,160},{224,192},{256... | collective-permute-start | bytes 393224 | tf_op jit(solution)/shard_map/ppermute | solution.py:18
Sparse Core Ops, SparseCore 0:
  90.3 121.4 reduce-scatter.1
